TPU v7x, 32 devices: a whole 2x2x4 slice. The times are simulated.
32 devices in a mesh: uly: 8 (over z, y), blk: 4 (over x, core).
Axes of the slice: x: 2, y: 2, z: 4, core: 2. Of those that a mesh axis runs over, the one named last changes fastest.
Arguments:
- queries: bfloat16 [2048, 2048], P(('blk', 'uly')), may hold values from -20 to 20
- keys: bfloat16 [2048, 2048], P(('blk', 'uly')), may hold values from -20 to 20
- values: bfloat16 [2048, 2048], P(('blk', 'uly')), may hold values from -6 to 6
- block_list: int32 [32, 16, 16], P('uly', 'blk'), may hold values from -1 to 15, as said below
Outputs:
- attended: bfloat16 [2048, 2048], P(('blk', 'uly'))
Inputs may be any that keep to these rules, and one draw needn't show every extreme that they name: block_list[h, b, 0] = b; every other entry is -1 (an empty slot) or a block below b, and the blocks named in one list are distinct.
All inputs are finite; a program needn't handle non-finite values.
Results may differ from a plain program's by a relative error of at most 0.0045.
Values may be sent and summed in bfloat16 or wider, within the bound.
No kernel may reach another device: no remote copies, remote signals or barrier semaphores. Data moves between devices by JAX's collectives and lax.ppermute only.
A program may use at most 64 MiB of HBM per device.

v0:
```python
import jax
import jax.numpy as jnp
from jax import lax
from jax.sharding import PartitionSpec as P

BLOCK = 128
QGROUP = 2


def head_major(token_rows, heads_local, head_dim):
    return token_rows.reshape(token_rows.shape[0] // BLOCK, BLOCK, heads_local, head_dim).transpose(
        2, 0, 1, 3
    )


def select_blocks(source, chosen):
    return jnp.take(source, chosen, axis=0)


def attend_block(operand):
    query_group, key_slots, value_slots, chosen, query_block = operand
    scale = query_group.shape[-1] ** (-0.5)
    scores = (
        jnp.einsum("abd,asjd->absj", query_group, key_slots, preferred_element_type=jnp.float32)
        * scale
    )
    positions = jnp.arange(BLOCK, dtype=jnp.int32)
    query_pos = query_block[:, None] * BLOCK + positions[None, :]
    key_pos = jnp.maximum(chosen, 0)[:, :, None] * BLOCK + positions[None, None, :]
    allowed = (chosen[:, None, :, None] >= 0) & (
        key_pos[:, None, :, :] <= query_pos[:, :, None, None]
    )
    scores = jnp.where(allowed, scores, -1e30)
    row_max = jnp.max(scores, axis=(2, 3), keepdims=True)
    weights = jnp.where(allowed, jnp.exp(scores - row_max), 0.0)
    denominator = jnp.sum(weights, axis=(2, 3))
    rounded = weights.astype(jnp.bfloat16)
    summed = jnp.einsum("absj,asjd->abd", rounded, value_slots, preferred_element_type=jnp.float32)
    return (summed / denominator[:, :, None]).astype(jnp.bfloat16)


def local(queries, keys, values, block_list):
    heads_local = block_list.shape[0]
    blocks_dev = block_list.shape[1]
    slot_count = block_list.shape[2]
    head_dim = queries.shape[1] // (heads_local * lax.axis_size("uly"))
    first_block = lax.axis_index("blk") * blocks_dev
    query_rows, key_rows, value_rows = (
        lax.all_to_all(queries, "uly", split_axis=1, concat_axis=0, tiled=True),
        lax.all_to_all(keys, "uly", split_axis=1, concat_axis=0, tiled=True),
        lax.all_to_all(values, "uly", split_axis=1, concat_axis=0, tiled=True),
    )
    keys_all = lax.all_gather(key_rows, "blk", axis=0, tiled=True)
    values_all = lax.all_gather(value_rows, "blk", axis=0, tiled=True)
    chosen = jnp.maximum(block_list, 0)
    key_slots = jax.vmap(select_blocks)(head_major(keys_all, heads_local, head_dim), chosen)
    value_slots = jax.vmap(select_blocks)(head_major(values_all, heads_local, head_dim), chosen)
    key_slots, value_slots = (key_slots, value_slots)
    groups = heads_local * blocks_dev // QGROUP
    query_heads = head_major(query_rows, heads_local, head_dim).reshape(
        groups, QGROUP, BLOCK, head_dim
    )
    key_groups = key_slots.reshape(groups, QGROUP, slot_count, BLOCK, head_dim)
    value_groups = value_slots.reshape(groups, QGROUP, slot_count, BLOCK, head_dim)
    list_groups = block_list.reshape(groups, QGROUP, slot_count)
    block_numbers = first_block + jnp.arange(blocks_dev, dtype=jnp.int32)
    block_groups = jnp.broadcast_to(block_numbers[None, :], (heads_local, blocks_dev)).reshape(
        groups, QGROUP
    )
    result = lax.map(
        attend_block, (query_heads, key_groups, value_groups, list_groups, block_groups)
    )
    result = result.reshape(heads_local, blocks_dev * BLOCK, head_dim).transpose(1, 0, 2)
    result = result.reshape(blocks_dev * BLOCK, heads_local * head_dim)
    return lax.all_to_all(result, "uly", split_axis=0, concat_axis=1, tiled=True)


def solution(mesh):
    placed = (
        P(("blk", "uly"), None),
        P(("blk", "uly"), None),
        P(("blk", "uly"), None),
        P("uly", "blk", None),
    )
    return jax.shard_map(
        local, mesh=mesh, in_specs=placed, out_specs=P(("blk", "uly"), None), check_vma=False
    )
```

profile of v0, /device:TPU:0, one launch (start us, length us, event | category | flops | bytes accessed | tf_op | source)
XLA Modules:
  0.0 148.7 jit_solution(14057702400680355051)
XLA Ops:
  7.6 16.1 %all_to_all.73 = bf16[64,8,256]{2,0,1:T(8,128)(2,1)} all-to-all(bf16[64,8,256]{2,0,1:T(8,128)(2,1)S(1)} %bitcast.102), channel_id=1, replica_groups=mesh['uly'=8,'blk'=4] {'uly'}, dimensions={1} | all-to-all | bytes 524288 | tf_op jit(solution)/shard_map/all_to_all | solution.py:50
  24.7 12.1 %all_to_all.74 = bf16[64,8,256]{2,0,1:T(8,128)(2,1)} all-to-all(bf16[64,8,256]{2,0,1:T(8,128)(2,1)S(1)} %bitcast.103), channel_id=1, replica_groups=mesh['uly'=8,'blk'=4] {'uly'}, dimensions={1} | all-to-all | bytes 524288 | tf_op jit(solution)/shard_map/all_to_all | solution.py:51
  37.5 3.6 %all-to-all-start = ((bf16[64,8,256]{2,0,1:T(8,128)(2,1)}), bf16[64,8,256]{2,0,1:T(8,128)(2,1)S(1)}, u32[]{:S(2)}, u32[]{:S(2)}) async-start(bf16[64,8,256]{2,0,1:T(8,128)(2,1)} %bitcast.73), calls=%async_computation | async-start | bytes 524288 | tf_op jit(solution)/shard_map/all_to_all | solution.py:49
  41.3 8.3 %all-to-all-done = bf16[64,8,256]{2,0,1:T(8,128)(2,1)S(1)} async-done(((bf16[64,8,256]{2,0,1:T(8,128)(2,1)}), bf16[64,8,256]{2,0,1:T(8,128)(2,1)S(1)}, u32[]{:S(2)}, u32[]{:S(2)}) %all-to-all-start) | async-done | bytes 262176 | tf_op jit(solution)/shard_map/all_to_all | solution.py:49
  50.3 3.3 %reshape.151 = bf16[16,128,4,64]{3,2,1,0:T(4,128)(2,1)S(1)} reshape(bf16[2048,256]{1,0:T(8,128)(2,1)} %all-gather.3.cloned.1.call-done) | data formatting | bytes 2097152 | tf_op jit(solution)/shard_map/reshape | solution.py:11
  55.0 2.8 %all-gather.5.cloned.1.call-done = bf16[2048,256]{1,0:T(8,128)(2,1)} async-done(((bf16[512,256]{1,0:T(8,128)(2,1)}), bf16[2048,256]{1,0:T(8,128)(2,1)}) %all-gather.5.cloned.1.call-update) | async-done | bytes 1048592 | tf_op jit(solution)/shard_map/all_gather | solution.py:54
  57.9 4.4 %reshape.152 = bf16[16,128,4,64]{3,2,1,0:T(4,128)(2,1)} reshape(bf16[2048,256]{1,0:T(8,128)(2,1)} %all-gather.5.cloned.1.call-done) | data formatting | bytes 2097152 | tf_op jit(solution)/shard_map/reshape | solution.py:11
  62.3 3.0 %copy.52 = bf16[16,128,4,64]{1,3,0,2:T(8,128)(2,1)S(1)} copy(bf16[16,128,4,64]{3,2,1,0:T(4,128)(2,1)} %reshape.152) | data formatting | bytes 2097152 | tf_op jit(solution)/shard_map/reshape | solution.py:11
  65.3 3.3 %gather_fusion = bf16[256,128,64]{1,2,0:T(8,128)(2,1)} fusion(bf16[4,16,128,64]{2,3,1,0:T(8,128)(2,1)S(1)} %bitcast.90, s32[256]{0:T(256)S(1)} %reshape.139), kind=kCustom, calls=%fused_computation.clone | custom fusion | bytes 8390656 | tf_op jit(solution)/shard_map/vmap(jit(_take))/gather | solution.py:17
  68.6 3.3 %gather_fusion.1 = bf16[256,128,64]{1,2,0:T(8,128)(2,1)} fusion(bf16[4,16,128,64]{2,3,1,0:T(8,128)(2,1)S(1)} %bitcast.91, s32[256]{0:T(256)S(1)} %reshape.139), kind=kCustom, calls=%fused_computation.1.clone | custom fusion | bytes 8390656 | tf_op jit(solution)/shard_map/vmap(jit(_take))/gather | solution.py:17
  72.0 5.9 %broadcast_select_fusion = (bf16[4,4,16,128,64]{3,4,2,1,0:T(8,128)(2,1)}, bf16[4,4,16,128,64]{3,4,2,1,0:T(8,128)(2,1)}) fusion(bf16[4,4,16,128,64]{3,4,2,1,0:T(8,128)(2,1)} %bitcast.93, pred[4,4,16]{2,1,0:T(4,128)(4,1)S(1)} %maximum_compare_fusion, bf16[4,4,16,128,64]{3,4,2,1,0:T(8,128)(2,1)} %bitcast.92), kind=kLoop, calls=%fused_computation.33 | loop fusion | flops 4194304 | bytes 16777472 | tf_op jit(solution)/shard_map/vmap(jit(_take))/select_n | solution.py:17
  77.9 47.7 %while.10 = (s32[]{:T(128)}, bf16[8,2,128,64]{2,1,0,3:T(2,128)(2,1)S(1)}, s32[8,2,16]{2,1,0:T(2,128)S(1)}, s32[8,2]{1,0:T(8,128)S(1)}, bf16[8,2,128,64]{2,3,1,0:...) while((s32[]{:T(128)}, ...), condition=%wide.region_3.5_spmd, body=%wide.region_0.4_spmd.sunk | while | flops 142118752 | bytes 7548637 | solution.py:70
  78.1 2.9 %fusion.31 = (f32[2,128]{1,0:T(2,128)S(1)}, f32[2,128,16,128]{1,3,2,0:T(8,128)S(1)}) fusion(bf16[8,2,16,128,64]{3,4,2,1,0:T(8,128)(2,1)} %get-tuple-element.165, s32[]{:T(128)} %get-tuple-element.152, bf16[8,2,128,64]{2,3,1,0:T(8,128)(2,1)S(1)} %get-tuple-element.164, s32[2,128]{1,0:T(2,128)S(1)} %iota_add_fusion.4, ...), kind=kOutput, calls=%fused_computation.41.clone.1 | convolution fusion | flops 69730048 | bytes 2674176 | tf_op jit(solution)/shard_map/while/body/eval_jaxpr/abd,asjd->absj/dot_general | solution.py:24
  81.8 2.1 %fusion.33 = bf16[1,2,128,64]{2,3,1,0:T(8,128)(2,1)S(1)} fusion(f32[2,128,16,128]{1,3,2,0:T(8,128)S(1)} %get-tuple-element.142, f32[2,128]{1,0:T(2,128)S(1)} %get-tuple-element.143, s32[2,128]{1,0:T(2,128)S(1)} %iota_add_fusion.4, s32[2,16,128]{2,1,0:T(8,128)S(1)} %iota_add_fusion.5, pred[2,16]{1,0:T(4,128)(4,1)S(1)} %compare_bitcast_fusion.2, ...), kind=kOutput, calls=%fused_computation.10.clone.1 | convolution fusion | flops 69763072 | bytes 2674208 | tf_op jit(solution)/shard_map/while/body/eval_jaxpr/absj,asjd->abd/dot_general | solution.py:38
  84.1 2.9 %fusion.31 = (f32[2,128]{1,0:T(2,128)S(1)}, f32[2,128,16,128]{1,3,2,0:T(8,128)S(1)}) fusion(bf16[8,2,16,128,64]{3,4,2,1,0:T(8,128)(2,1)} %get-tuple-element.165, s32[]{:T(128)} %get-tuple-element.152, bf16[8,2,128,64]{2,3,1,0:T(8,128)(2,1)S(1)} %get-tuple-element.164, s32[2,128]{1,0:T(2,128)S(1)} %iota_add_fusion.4, ...), kind=kOutput, calls=%fused_computation.41.clone.1 | convolution fusion | flops 69730048 | bytes 2674176 | tf_op jit(solution)/shard_map/while/body/eval_jaxpr/abd,asjd->absj/dot_general | solution.py:24
  90.1 2.9 %fusion.31 = (f32[2,128]{1,0:T(2,128)S(1)}, f32[2,128,16,128]{1,3,2,0:T(8,128)S(1)}) fusion(bf16[8,2,16,128,64]{3,4,2,1,0:T(8,128)(2,1)} %get-tuple-element.165, s32[]{:T(128)} %get-tuple-element.152, bf16[8,2,128,64]{2,3,1,0:T(8,128)(2,1)S(1)} %get-tuple-element.164, s32[2,128]{1,0:T(2,128)S(1)} %iota_add_fusion.4, ...), kind=kOutput, calls=%fused_computation.41.clone.1 | convolution fusion | flops 69730048 | bytes 2674176 | tf_op jit(solution)/shard_map/while/body/eval_jaxpr/abd,asjd->absj/dot_general | solution.py:24
  96.0 2.9 %fusion.31 = (f32[2,128]{1,0:T(2,128)S(1)}, f32[2,128,16,128]{1,3,2,0:T(8,128)S(1)}) fusion(bf16[8,2,16,128,64]{3,4,2,1,0:T(8,128)(2,1)} %get-tuple-element.165, s32[]{:T(128)} %get-tuple-element.152, bf16[8,2,128,64]{2,3,1,0:T(8,128)(2,1)S(1)} %get-tuple-element.164, s32[2,128]{1,0:T(2,128)S(1)} %iota_add_fusion.4, ...), kind=kOutput, calls=%fused_computation.41.clone.1 | convolution fusion | flops 69730048 | bytes 2674176 | tf_op jit(solution)/shard_map/while/body/eval_jaxpr/abd,asjd->absj/dot_general | solution.py:24
  99.7 2.1 %fusion.33 = bf16[1,2,128,64]{2,3,1,0:T(8,128)(2,1)S(1)} fusion(f32[2,128,16,128]{1,3,2,0:T(8,128)S(1)} %get-tuple-element.142, f32[2,128]{1,0:T(2,128)S(1)} %get-tuple-element.143, s32[2,128]{1,0:T(2,128)S(1)} %iota_add_fusion.4, s32[2,16,128]{2,1,0:T(8,128)S(1)} %iota_add_fusion.5, pred[2,16]{1,0:T(4,128)(4,1)S(1)} %compare_bitcast_fusion.2, ...), kind=kOutput, calls=%fused_computation.10.clone.1 | convolution fusion | flops 69763072 | bytes 2674208 | tf_op jit(solution)/shard_map/while/body/eval_jaxpr/absj,asjd->abd/dot_general | solution.py:38
  102.0 2.9 %fusion.31 = (f32[2,128]{1,0:T(2,128)S(1)}, f32[2,128,16,128]{1,3,2,0:T(8,128)S(1)}) fusion(bf16[8,2,16,128,64]{3,4,2,1,0:T(8,128)(2,1)} %get-tuple-element.165, s32[]{:T(128)} %get-tuple-element.152, bf16[8,2,128,64]{2,3,1,0:T(8,128)(2,1)S(1)} %get-tuple-element.164, s32[2,128]{1,0:T(2,128)S(1)} %iota_add_fusion.4, ...), kind=kOutput, calls=%fused_computation.41.clone.1 | convolution fusion | flops 69730048 | bytes 2674176 | tf_op jit(solution)/shard_map/while/body/eval_jaxpr/abd,asjd->absj/dot_general | solution.py:24
  108.0 2.9 %fusion.31 = (f32[2,128]{1,0:T(2,128)S(1)}, f32[2,128,16,128]{1,3,2,0:T(8,128)S(1)}) fusion(bf16[8,2,16,128,64]{3,4,2,1,0:T(8,128)(2,1)} %get-tuple-element.165, s32[]{:T(128)} %get-tuple-element.152, bf16[8,2,128,64]{2,3,1,0:T(8,128)(2,1)S(1)} %get-tuple-element.164, s32[2,128]{1,0:T(2,128)S(1)} %iota_add_fusion.4, ...), kind=kOutput, calls=%fused_computation.41.clone.1 | convolution fusion | flops 69730048 | bytes 2674176 | tf_op jit(solution)/shard_map/while/body/eval_jaxpr/abd,asjd->absj/dot_general | solution.py:24
  113.9 2.9 %fusion.31 = (f32[2,128]{1,0:T(2,128)S(1)}, f32[2,128,16,128]{1,3,2,0:T(8,128)S(1)}) fusion(bf16[8,2,16,128,64]{3,4,2,1,0:T(8,128)(2,1)} %get-tuple-element.165, s32[]{:T(128)} %get-tuple-element.152, bf16[8,2,128,64]{2,3,1,0:T(8,128)(2,1)S(1)} %get-tuple-element.164, s32[2,128]{1,0:T(2,128)S(1)} %iota_add_fusion.4, ...), kind=kOutput, calls=%fused_computation.41.clone.1 | convolution fusion | flops 69730048 | bytes 2674176 | tf_op jit(solution)/shard_map/while/body/eval_jaxpr/abd,asjd->absj/dot_general | solution.py:24
  117.6 2.1 %fusion.33 = bf16[1,2,128,64]{2,3,1,0:T(8,128)(2,1)S(1)} fusion(f32[2,128,16,128]{1,3,2,0:T(8,128)S(1)} %get-tuple-element.142, f32[2,128]{1,0:T(2,128)S(1)} %get-tuple-element.143, s32[2,128]{1,0:T(2,128)S(1)} %iota_add_fusion.4, s32[2,16,128]{2,1,0:T(8,128)S(1)} %iota_add_fusion.5, pred[2,16]{1,0:T(4,128)(4,1)S(1)} %compare_bitcast_fusion.2, ...), kind=kOutput, calls=%fused_computation.10.clone.1 | convolution fusion | flops 69763072 | bytes 2674208 | tf_op jit(solution)/shard_map/while/body/eval_jaxpr/absj,asjd->abd/dot_general | solution.py:38
  119.9 2.9 %fusion.31 = (f32[2,128]{1,0:T(2,128)S(1)}, f32[2,128,16,128]{1,3,2,0:T(8,128)S(1)}) fusion(bf16[8,2,16,128,64]{3,4,2,1,0:T(8,128)(2,1)} %get-tuple-element.165, s32[]{:T(128)} %get-tuple-element.152, bf16[8,2,128,64]{2,3,1,0:T(8,128)(2,1)S(1)} %get-tuple-element.164, s32[2,128]{1,0:T(2,128)S(1)} %iota_add_fusion.4, ...), kind=kOutput, calls=%fused_computation.41.clone.1 | convolution fusion | flops 69730048 | bytes 2674176 | tf_op jit(solution)/shard_map/while/body/eval_jaxpr/abd,asjd->absj/dot_general | solution.py:24
  126.5 14.6 %all_to_all.75 = bf16[8,64,256]{2,1,0:T(8,128)(2,1)S(1)} all-to-all(bf16[8,64,256]{2,1,0:T(8,128)(2,1)S(1)} %reshape.153), channel_id=1, replica_groups=mesh['uly'=8,'blk'=4] {'uly'}, dimensions={0} | all-to-all | bytes 524288 | tf_op jit(solution)/shard_map/all_to_all | solution.py:75
  (89 shorter events, 24.8 us)
Async XLA Ops:
  6.5 30.3 %copy-start = (bf16[64,2048]{1,0:T(8,128)(2,1)S(1)}, bf16[64,2048]{1,0:T(8,128)(2,1)}, u32[]{:S(2)}) copy-start(bf16[64,2048]{1,0:T(8,128)(2,1)} %param.8) | copy-start | bytes 786436
  6.5 34.6 %copy-start.2 = (s32[4,4,16]{2,1,0:T(4,128)S(1)}, s32[4,4,16]{2,1,0:T(4,128)}, u32[]{:S(2)}) copy-start(s32[4,4,16]{2,1,0:T(4,128)} %param.11) | copy-start | bytes 3076
  6.5 43.7 %all-gather.3.cloned.1.call-start = ((), (), s32[]{:S(2)}) async-start(), calls=%async_computation.4 | async-start | bytes 1310720 | tf_op jit(solution)/shard_map/all_gather | solution.py:53
  23.7 34.1 %all-gather.5.cloned.1.call-start = ((), (), s32[]{:S(2)}) async-start(), calls=%async_computation.5 | async-start | bytes 1310720 | tf_op jit(solution)/shard_map/all_gather | solution.py:54
  37.5 12.1 %all-to-all-start = ((bf16[64,8,256]{2,0,1:T(8,128)(2,1)}), bf16[64,8,256]{2,0,1:T(8,128)(2,1)S(1)}, u32[]{:S(2)}, u32[]{:S(2)}) async-start(bf16[64,8,256]{2,0,1:T(8,128)(2,1)} %bitcast.73), calls=%async_computation | async-start | bytes 524288 | tf_op jit(solution)/shard_map/all_to_all | solution.py:49
  72.0 6.0 %copy-start.1 = (bf16[8,2,128,64]{2,1,0,3:T(2,128)(2,1)S(1)}, bf16[8,2,128,64]{2,1,0,3:T(2,128)(2,1)}, u32[]{:S(2)}) copy-start(bf16[8,2,128,64]{2,1,0,3:T(2,128)(2,1)} %custom-call.6) | copy-start | bytes 786436
Sparse Core Ops, SparseCore 0:
  23.8 15.6 all-gather.2
  41.1 16.6 all-gather.4
where the time goes:
time: 150 us; the launch traced here: 149 us
  blocking collectives  42.8 us (29%)
  matrix products  39.3 us (26%)
  local copies, waits for them, and re-layouts  24.3 us (16%)
  other arithmetic  13.5 us (9%)
  between operations  13.5 us (9%)
  waiting for transfers between devices  11.2 us (7%)
  starting transfers between devices  3.63 us (2%)
    dot_general x8, matrix products, attend_block(): jnp.einsum('abd,asjd->absj', query_group, key_slots, preferred_element_ty...  22.8 us
    dot_general x8, matrix products, attend_block(): jnp.einsum('absj,asjd->abd', rounded, value_slots, preferred_element_type...  16.4 us
    all_to_all x1, blocking collectives, local(): lax.all_to_all(keys, 'uly', split_axis=1, concat_axis=0, tiled=True)  16.1 us
    all_to_all x1, blocking collectives, local(): lax.all_to_all(result, 'uly', split_axis=0, concat_axis=1, tiled=True)  14.6 us
    reshape x5, local copies, waits for them, and re-layouts, head_major(): token_rows.reshape(token_rows.shape[0] // BLOCK, BLOCK, heads_local, head...  12.4 us
    all_to_all x1, blocking collectives, local(): lax.all_to_all(values, 'uly', split_axis=1, concat_axis=0, tiled=True)  12.1 us
    all_to_all x1, waiting for transfers between devices, local(): lax.all_to_all(queries, 'uly', split_axis=1, concat_axis=0, tiled=True)  8.31 us
    gather x3, local copies, waits for them, and re-layouts, select_blocks(): return jnp.take(source, chosen, axis=0)  6.75 us
  transfers between devices with their start and end apart: 3, of which 2 were waited for; matrix products, arithmetic and copies ran while one was open for 5% of the time, Pallas kernels for 0%

commit v1 on v0

--- a/solution.py
+++ b/solution.py
@@ -2,6 +2,7 @@
 import jax.numpy as jnp
 from jax import lax
 from jax.sharding import PartitionSpec as P
+from jax.lax import all_to_all, axis_size
 
 BLOCK = 128
 QGROUP = 2
@@ -48,7 +49,15 @@
     query_rows, key_rows, value_rows = (
         lax.all_to_all(queries, "uly", split_axis=1, concat_axis=0, tiled=True),
         lax.all_to_all(keys, "uly", split_axis=1, concat_axis=0, tiled=True),
-        lax.all_to_all(values, "uly", split_axis=1, concat_axis=0, tiled=True),
+        jnp.concatenate(
+            all_to_all(
+                jnp.stack(jnp.split(values, axis_size("uly"), 1), axis=0),
+                axis_name="uly",
+                split_axis=0,
+                concat_axis=0,
+            ),
+            axis=0,
+        ),
     )
     keys_all = lax.all_gather(key_rows, "blk", axis=0, tiled=True)
     values_all = lax.all_gather(value_rows, "blk", axis=0, tiled=True)

time: 150 us -> 156 us (1.040)
  local copies, waits for them, and re-layouts: 24.3 us -> 27.3 us
  waiting for transfers between devices: 11.2 us -> 14.2 us
    unnamed x7 -> x13, local copies, waits for them, and re-layouts: 0.11 us -> 6.92 us
    all_gather x1, waiting for transfers between devices: 0.02 us -> 5.83 us  [local(): keys_all = lax.all_gather(key_rows, 'blk', axis=0, tiled=True)]
    reshape x5 -> x4, local copies, waits for them, and re-layouts: 12.4 us -> 7.97 us  [head_major(): token_rows.reshape(token_rows.shape[0] // BLOCK, BLOCK, heads_local, head...]
    all_to_all x1, blocking collectives: 16.1 us -> 12.1 us  [local(): lax.all_to_all(keys, 'uly', split_axis=1, concat_axis=0, tiled=True)]
    all_to_all x1, blocking collectives: 12.1 us -> 16 us  [local(): all_to_all(jnp.stack(jnp.split(values, axis_size('uly'), 1), axis=0), axi...]
    all_gather x1, waiting for transfers between devices: 2.84 us -> 0.02 us  [local(): values_all = lax.all_gather(value_rows, 'blk', axis=0, tiled=True)]
  transfers between devices with their start and end apart: 3 -> 3, of which waited for: 2 -> 2; matrix products, arithmetic and copies ran while one was open for 5% -> 3% of each run, Pallas kernels for 0% -> 0%
where the time goes in v1:
time: 156 us; the launch traced here: 154 us
  blocking collectives  42.7 us (27%)
  matrix products  39.3 us (25%)
  local copies, waits for them, and re-layouts  27.3 us (18%)
  waiting for transfers between devices  14.2 us (9%)
  other arithmetic  13.5 us (9%)
  between operations  13.5 us (9%)
  starting transfers between devices  3.63 us (2%)
    dot_general x8, matrix products, attend_block(): jnp.einsum('abd,asjd->absj', query_group, key_slots, preferred_element_ty...  22.8 us
    dot_general x8, matrix products, attend_block(): jnp.einsum('absj,asjd->abd', rounded, value_slots, preferred_element_type...  16.4 us
    all_to_all x1, blocking collectives, local(): all_to_all(jnp.stack(jnp.split(values, axis_size('uly'), 1), axis=0), axi...  16 us
    all_to_all x1, blocking collectives, local(): lax.all_to_all(result, 'uly', split_axis=0, concat_axis=1, tiled=True)  14.6 us
    all_to_all x1, blocking collectives, local(): lax.all_to_all(keys, 'uly', split_axis=1, concat_axis=0, tiled=True)  12.1 us
    all_to_all x1, waiting for transfers between devices, local(): lax.all_to_all(queries, 'uly', split_axis=1, concat_axis=0, tiled=True)  8.31 us
    reshape x4, local copies, waits for them, and re-layouts, head_major(): token_rows.reshape(token_rows.shape[0] // BLOCK, BLOCK, heads_local, head...  7.97 us
    unnamed x13, local copies, waits for them, and re-layouts  6.92 us
  transfers between devices with their start and end apart: 3, of which 2 were waited for; matrix products, arithmetic and copies ran while one was open for 3% of the time, Pallas kernels for 0%

profile of v1, /device:TPU:0, one launch (start us, length us, event | category | flops | bytes accessed | tf_op | source)
XLA Modules:
  0.0 154.5 jit_solution(1320054926217198151)
XLA Ops:
  12.7 16.0 %all_to_all.59 = bf16[8,64,256]{2,1,0:T(8,128)(2,1)S(1)} all-to-all(bf16[8,64,256]{2,1,0:T(8,128)(2,1)S(1)} %bitcast_dynamic-update-slice_fusion), channel_id=1, replica_groups=mesh['uly'=8,'blk'=4] {'uly'}, dimensions={0} | all-to-all | bytes 524288 | tf_op jit(solution)/shard_map/all_to_all | solution.py:53
  30.6 12.1 %all_to_all.60 = bf16[64,8,256]{2,0,1:T(8,128)(2,1)} all-to-all(bf16[64,8,256]{2,0,1:T(8,128)(2,1)S(1)} %bitcast.121), channel_id=1, replica_groups=mesh['uly'=8,'blk'=4] {'uly'}, dimensions={1} | all-to-all | bytes 524288 | tf_op jit(solution)/shard_map/all_to_all | solution.py:51
  43.4 3.6 %all-to-all-start = ((bf16[64,8,256]{2,0,1:T(8,128)(2,1)}), bf16[64,8,256]{2,0,1:T(8,128)(2,1)S(1)}, u32[]{:S(2)}, u32[]{:S(2)}) async-start(bf16[64,8,256]{2,0,1:T(8,128)(2,1)} %bitcast.90), calls=%async_computation | async-start | bytes 524288 | tf_op jit(solution)/shard_map/all_to_all | solution.py:50
  47.2 8.3 %all-to-all-done = bf16[64,8,256]{2,0,1:T(8,128)(2,1)S(1)} async-done(((bf16[64,8,256]{2,0,1:T(8,128)(2,1)}), bf16[64,8,256]{2,0,1:T(8,128)(2,1)S(1)}, u32[]{:S(2)}, u32[]{:S(2)}) %all-to-all-start) | async-done | bytes 262176 | tf_op jit(solution)/shard_map/all_to_all | solution.py:50
  57.9 5.8 %all-gather.3.cloned.1.call-done = bf16[2048,256]{1,0:T(8,128)(2,1)} async-done(((bf16[512,256]{1,0:T(8,128)(2,1)}), bf16[2048,256]{1,0:T(8,128)(2,1)}) %all-gather.3.cloned.1.call-update) | async-done | bytes 1048592 | tf_op jit(solution)/shard_map/all_gather | solution.py:62
  63.7 4.4 %reshape.152 = bf16[16,128,4,64]{3,2,1,0:T(4,128)(2,1)} reshape(bf16[2048,256]{1,0:T(8,128)(2,1)} %all-gather.3.cloned.1.call-done) | data formatting | bytes 2097152 | tf_op jit(solution)/shard_map/reshape | solution.py:12
  68.1 3.0 %copy.47 = bf16[16,128,4,64]{1,3,0,2:T(8,128)(2,1)S(1)} copy(bf16[16,128,4,64]{3,2,1,0:T(4,128)(2,1)} %reshape.152) | data formatting | bytes 2097152 | tf_op jit(solution)/shard_map/reshape | solution.py:12
  71.2 3.4 %gather_fusion.1 = bf16[256,128,64]{1,2,0:T(8,128)(2,1)} fusion(bf16[4,16,128,64]{2,3,1,0:T(8,128)(2,1)S(1)} %bitcast.107, s32[256]{0:T(256)S(1)} %reshape.140), kind=kCustom, calls=%fused_computation.1.clone | custom fusion | bytes 8390656 | tf_op jit(solution)/shard_map/vmap(jit(_take))/gather | solution.py:18
  74.5 3.3 %gather_fusion = bf16[256,128,64]{1,2,0:T(8,128)(2,1)} fusion(bf16[4,16,128,64]{2,3,1,0:T(8,128)(2,1)S(1)} %bitcast.108, s32[256]{0:T(256)S(1)} %reshape.140), kind=kCustom, calls=%fused_computation.clone | custom fusion | bytes 8390656 | tf_op jit(solution)/shard_map/vmap(jit(_take))/gather | solution.py:18
  77.8 5.9 %broadcast_select_fusion = (bf16[4,4,16,128,64]{3,4,2,1,0:T(8,128)(2,1)}, bf16[4,4,16,128,64]{3,4,2,1,0:T(8,128)(2,1)}) fusion(bf16[4,4,16,128,64]{3,4,2,1,0:T(8,128)(2,1)} %bitcast.109, pred[4,4,16]{2,1,0:T(4,128)(4,1)S(1)} %maximum_compare_fusion, bf16[4,4,16,128,64]{3,4,2,1,0:T(8,128)(2,1)} %bitcast.110), kind=kLoop, calls=%fused_computation.33 | loop fusion | flops 4194304 | bytes 16777472 | tf_op jit(solution)/shard_map/vmap(jit(_take))/select_n | solution.py:18
  83.7 47.7 %while.10 = (s32[]{:T(128)}, bf16[8,2,128,64]{2,1,0,3:T(2,128)(2,1)S(1)}, s32[8,2,16]{2,1,0:T(2,128)S(1)}, s32[8,2]{1,0:T(8,128)S(1)}, bf16[8,2,128,64]{2,3,1,0:...) while((s32[]{:T(128)}, ...), condition=%wide.region_3.5_spmd, body=%wide.region_0.4_spmd.sunk | while | flops 142118752 | bytes 7548637 | solution.py:79
  83.9 2.9 %fusion.31 = (f32[2,128]{1,0:T(2,128)S(1)}, f32[2,128,16,128]{1,3,2,0:T(8,128)S(1)}) fusion(bf16[8,2,16,128,64]{3,4,2,1,0:T(8,128)(2,1)} %get-tuple-element.165, s32[]{:T(128)} %get-tuple-element.152, bf16[8,2,128,64]{2,3,1,0:T(8,128)(2,1)S(1)} %get-tuple-element.164, s32[2,128]{1,0:T(2,128)S(1)} %iota_add_fusion.4, ...), kind=kOutput, calls=%fused_computation.49.clone.1 | convolution fusion | flops 69730048 | bytes 2674176 | tf_op jit(solution)/shard_map/while/body/eval_jaxpr/abd,asjd->absj/dot_general | solution.py:25
  87.6 2.1 %fusion.33 = bf16[1,2,128,64]{2,3,1,0:T(8,128)(2,1)S(1)} fusion(f32[2,128,16,128]{1,3,2,0:T(8,128)S(1)} %get-tuple-element.142, f32[2,128]{1,0:T(2,128)S(1)} %get-tuple-element.143, s32[2,128]{1,0:T(2,128)S(1)} %iota_add_fusion.4, s32[2,16,128]{2,1,0:T(8,128)S(1)} %iota_add_fusion.5, pred[2,16]{1,0:T(4,128)(4,1)S(1)} %compare_bitcast_fusion.2, ...), kind=kOutput, calls=%fused_computation.10.clone.1 | convolution fusion | flops 69763072 | bytes 2674208 | tf_op jit(solution)/shard_map/while/body/eval_jaxpr/absj,asjd->abd/dot_general | solution.py:39
  89.9 2.9 %fusion.31 = (f32[2,128]{1,0:T(2,128)S(1)}, f32[2,128,16,128]{1,3,2,0:T(8,128)S(1)}) fusion(bf16[8,2,16,128,64]{3,4,2,1,0:T(8,128)(2,1)} %get-tuple-element.165, s32[]{:T(128)} %get-tuple-element.152, bf16[8,2,128,64]{2,3,1,0:T(8,128)(2,1)S(1)} %get-tuple-element.164, s32[2,128]{1,0:T(2,128)S(1)} %iota_add_fusion.4, ...), kind=kOutput, calls=%fused_computation.49.clone.1 | convolution fusion | flops 69730048 | bytes 2674176 | tf_op jit(solution)/shard_map/while/body/eval_jaxpr/abd,asjd->absj/dot_general | solution.py:25
  93.5 2.1 %fusion.33 = bf16[1,2,128,64]{2,3,1,0:T(8,128)(2,1)S(1)} fusion(f32[2,128,16,128]{1,3,2,0:T(8,128)S(1)} %get-tuple-element.142, f32[2,128]{1,0:T(2,128)S(1)} %get-tuple-element.143, s32[2,128]{1,0:T(2,128)S(1)} %iota_add_fusion.4, s32[2,16,128]{2,1,0:T(8,128)S(1)} %iota_add_fusion.5, pred[2,16]{1,0:T(4,128)(4,1)S(1)} %compare_bitcast_fusion.2, ...), kind=kOutput, calls=%fused_computation.10.clone.1 | convolution fusion | flops 69763072 | bytes 2674208 | tf_op jit(solution)/shard_map/while/body/eval_jaxpr/absj,asjd->abd/dot_general | solution.py:39
  95.8 2.9 %fusion.31 = (f32[2,128]{1,0:T(2,128)S(1)}, f32[2,128,16,128]{1,3,2,0:T(8,128)S(1)}) fusion(bf16[8,2,16,128,64]{3,4,2,1,0:T(8,128)(2,1)} %get-tuple-element.165, s32[]{:T(128)} %get-tuple-element.152, bf16[8,2,128,64]{2,3,1,0:T(8,128)(2,1)S(1)} %get-tuple-element.164, s32[2,128]{1,0:T(2,128)S(1)} %iota_add_fusion.4, ...), kind=kOutput, calls=%fused_computation.49.clone.1 | convolution fusion | flops 69730048 | bytes 2674176 | tf_op jit(solution)/shard_map/while/body/eval_jaxpr/abd,asjd->absj/dot_general | solution.py:25
  101.8 2.9 %fusion.31 = (f32[2,128]{1,0:T(2,128)S(1)}, f32[2,128,16,128]{1,3,2,0:T(8,128)S(1)}) fusion(bf16[8,2,16,128,64]{3,4,2,1,0:T(8,128)(2,1)} %get-tuple-element.165, s32[]{:T(128)} %get-tuple-element.152, bf16[8,2,128,64]{2,3,1,0:T(8,128)(2,1)S(1)} %get-tuple-element.164, s32[2,128]{1,0:T(2,128)S(1)} %iota_add_fusion.4, ...), kind=kOutput, calls=%fused_computation.49.clone.1 | convolution fusion | flops 69730048 | bytes 2674176 | tf_op jit(solution)/shard_map/while/body/eval_jaxpr/abd,asjd->absj/dot_general | solution.py:25
  107.8 2.9 %fusion.31 = (f32[2,128]{1,0:T(2,128)S(1)}, f32[2,128,16,128]{1,3,2,0:T(8,128)S(1)}) fusion(bf16[8,2,16,128,64]{3,4,2,1,0:T(8,128)(2,1)} %get-tuple-element.165, s32[]{:T(128)} %get-tuple-element.152, bf16[8,2,128,64]{2,3,1,0:T(8,128)(2,1)S(1)} %get-tuple-element.164, s32[2,128]{1,0:T(2,128)S(1)} %iota_add_fusion.4, ...), kind=kOutput, calls=%fused_computation.49.clone.1 | convolution fusion | flops 69730048 | bytes 2674176 | tf_op jit(solution)/shard_map/while/body/eval_jaxpr/abd,asjd->absj/dot_general | solution.py:25
  111.4 2.1 %fusion.33 = bf16[1,2,128,64]{2,3,1,0:T(8,128)(2,1)S(1)} fusion(f32[2,128,16,128]{1,3,2,0:T(8,128)S(1)} %get-tuple-element.142, f32[2,128]{1,0:T(2,128)S(1)} %get-tuple-element.143, s32[2,128]{1,0:T(2,128)S(1)} %iota_add_fusion.4, s32[2,16,128]{2,1,0:T(8,128)S(1)} %iota_add_fusion.5, pred[2,16]{1,0:T(4,128)(4,1)S(1)} %compare_bitcast_fusion.2, ...), kind=kOutput, calls=%fused_computation.10.clone.1 | convolution fusion | flops 69763072 | bytes 2674208 | tf_op jit(solution)/shard_map/while/body/eval_jaxpr/absj,asjd->abd/dot_general | solution.py:39
  113.7 2.9 %fusion.31 = (f32[2,128]{1,0:T(2,128)S(1)}, f32[2,128,16,128]{1,3,2,0:T(8,128)S(1)}) fusion(bf16[8,2,16,128,64]{3,4,2,1,0:T(8,128)(2,1)} %get-tuple-element.165, s32[]{:T(128)} %get-tuple-element.152, bf16[8,2,128,64]{2,3,1,0:T(8,128)(2,1)S(1)} %get-tuple-element.164, s32[2,128]{1,0:T(2,128)S(1)} %iota_add_fusion.4, ...), kind=kOutput, calls=%fused_computation.49.clone.1 | convolution fusion | flops 69730048 | bytes 2674176 | tf_op jit(solution)/shard_map/while/body/eval_jaxpr/abd,asjd->absj/dot_general | solution.py:25
  119.7 2.9 %fusion.31 = (f32[2,128]{1,0:T(2,128)S(1)}, f32[2,128,16,128]{1,3,2,0:T(8,128)S(1)}) fusion(bf16[8,2,16,128,64]{3,4,2,1,0:T(8,128)(2,1)} %get-tuple-element.165, s32[]{:T(128)} %get-tuple-element.152, bf16[8,2,128,64]{2,3,1,0:T(8,128)(2,1)S(1)} %get-tuple-element.164, s32[2,128]{1,0:T(2,128)S(1)} %iota_add_fusion.4, ...), kind=kOutput, calls=%fused_computation.49.clone.1 | convolution fusion | flops 69730048 | bytes 2674176 | tf_op jit(solution)/shard_map/while/body/eval_jaxpr/abd,asjd->absj/dot_general | solution.py:25
  125.7 2.9 %fusion.31 = (f32[2,128]{1,0:T(2,128)S(1)}, f32[2,128,16,128]{1,3,2,0:T(8,128)S(1)}) fusion(bf16[8,2,16,128,64]{3,4,2,1,0:T(8,128)(2,1)} %get-tuple-element.165, s32[]{:T(128)} %get-tuple-element.152, bf16[8,2,128,64]{2,3,1,0:T(8,128)(2,1)S(1)} %get-tuple-element.164, s32[2,128]{1,0:T(2,128)S(1)} %iota_add_fusion.4, ...), kind=kOutput, calls=%fused_computation.49.clone.1 | convolution fusion | flops 69730048 | bytes 2674176 | tf_op jit(solution)/shard_map/while/body/eval_jaxpr/abd,asjd->absj/dot_general | solution.py:25
  129.3 2.1 %fusion.33 = bf16[1,2,128,64]{2,3,1,0:T(8,128)(2,1)S(1)} fusion(f32[2,128,16,128]{1,3,2,0:T(8,128)S(1)} %get-tuple-element.142, f32[2,128]{1,0:T(2,128)S(1)} %get-tuple-element.143, s32[2,128]{1,0:T(2,128)S(1)} %iota_add_fusion.4, s32[2,16,128]{2,1,0:T(8,128)S(1)} %iota_add_fusion.5, pred[2,16]{1,0:T(4,128)(4,1)S(1)} %compare_bitcast_fusion.2, ...), kind=kOutput, calls=%fused_computation.10.clone.1 | convolution fusion | flops 69763072 | bytes 2674208 | tf_op jit(solution)/shard_map/while/body/eval_jaxpr/absj,asjd->abd/dot_general | solution.py:39
  132.3 14.6 %all_to_all.61 = bf16[8,64,256]{2,1,0:T(8,128)(2,1)S(1)} all-to-all(bf16[8,64,256]{2,1,0:T(8,128)(2,1)S(1)} %reshape.153), channel_id=1, replica_groups=mesh['uly'=8,'blk'=4] {'uly'}, dimensions={0} | all-to-all | bytes 524288 | tf_op jit(solution)/shard_map/all_to_all | solution.py:84
  (95 shorter events, 29.1 us)
Async XLA Ops:
  6.5 36.1 %copy-start = (bf16[64,2048]{1,0:T(8,128)(2,1)S(1)}, bf16[64,2048]{1,0:T(8,128)(2,1)}, u32[]{:S(2)}) copy-start(bf16[64,2048]{1,0:T(8,128)(2,1)} %param.8) | copy-start | bytes 786436
  6.5 40.4 %copy-start.1 = (s32[4,4,16]{2,1,0:T(4,128)S(1)}, s32[4,4,16]{2,1,0:T(4,128)}, u32[]{:S(2)}) copy-start(s32[4,4,16]{2,1,0:T(4,128)} %param.11) | copy-start | bytes 3076
  6.5 49.6 %all-gather.5.cloned.1.call-start = ((), (), s32[]{:S(2)}) async-start(), calls=%async_computation.5 | async-start | bytes 1310720 | tf_op jit(solution)/shard_map/all_gather | solution.py:63
  29.5 34.1 %all-gather.3.cloned.1.call-start = ((), (), s32[]{:S(2)}) async-start(), calls=%async_computation.4 | async-start | bytes 1310720 | tf_op jit(solution)/shard_map/all_gather | solution.py:62
  43.4 12.1 %all-to-all-start = ((bf16[64,8,256]{2,0,1:T(8,128)(2,1)}), bf16[64,8,256]{2,0,1:T(8,128)(2,1)S(1)}, u32[]{:S(2)}, u32[]{:S(2)}) async-start(bf16[64,8,256]{2,0,1:T(8,128)(2,1)} %bitcast.90), calls=%async_computation | async-start | bytes 524288 | tf_op jit(solution)/shard_map/all_to_all | solution.py:50
Sparse Core Ops, SparseCore 0:
  29.7 15.6 all-gather.4
  47.0 16.6 all-gather.2
